TPU v7x, 256 devices: a whole 4x4x8 slice. The times are simulated.
256 devices in a mesh: row: 32 (over z_lo, x, core), rhs: 8 (over y, z_hi).
Axes of the slice: x: 4, y: 4, z: 8 (z_hi: 2, z_lo: 4; z = z_hi * 4 + z_lo), core: 2. Of those that a mesh axis runs over, the one named last changes fastest.
Arguments:
- rhs_in: float32 [2, 1024, 16384], P(None, ('rhs', 'row')), may hold values from -6 to 6
- pivots: int32 [16384], replicated, may hold values from 0 to 16383, each once
- owners: int32 [32], replicated, may hold values from 0 to 31, each once
- panel_first: float32 [2, 16384, 512], P(None, 'row'), may hold values from -0.1875 to 0.1875
- panel_second: float32 [2, 16384, 512], P(None, 'row'), may hold values from -0.1875 to 0.1875
- inverse_first: float32 [2, 512, 512], replicated, may hold values from -0.1875 to 0.1875
- inverse_second: float32 [2, 512, 512], replicated, may hold values from -0.1875 to 0.1875
Outputs:
- solved_rhs: float32 [2, 1024, 16384], P(None, 'rhs', 'row')
Inputs may be any that keep to these rules, and one draw needn't show every extreme that they name: `pivots`: each row number occurs once. `owners`: each device index along row occurs once.
All inputs are finite; a program needn't handle non-finite values.
Results may differ from a plain program's by a relative error of at most 0.0001.
Values sent between devices are 32-bit elements; how exact they have to be, the bound alone decides.
No kernel may reach another device: no remote copies, remote signals or barrier semaphores. Data moves between devices by JAX's collectives and lax.ppermute only.
A program may use at most 128 MiB of HBM per device.

v0:
```python
import jax
import jax.numpy as jnp
from jax import lax
from jax.sharding import PartitionSpec as P


def broadcast(shard, axis, root):
    mine = lax.axis_index(axis) == root
    return lax.psum(jnp.where(mine, shard, jnp.zeros_like(shard)), axis)


def complex_product(operand, matrix):
    contract = (((1,), (1,)), ((), ()))

    def multiply(first, second):
        return lax.dot_general(
            first,
            second,
            contract,
            precision=lax.Precision.HIGHEST,
            preferred_element_type=jnp.float32,
        )

    real_part = multiply(operand[0], matrix[0]) - multiply(operand[1], matrix[1])
    imag_part = multiply(operand[0], matrix[1]) + multiply(operand[1], matrix[0])
    return jnp.stack([real_part, imag_part])


def shards(rhs_in, pivots, owners, panel_first, panel_second, inverse_first, inverse_second):
    blocks = owners.shape[0]
    block_size = panel_first.shape[2]
    slot_block = jnp.zeros((blocks,), jnp.int32).at[owners].set(jnp.arange(blocks, dtype=jnp.int32))
    row_index = (
        slot_block[:, None] * block_size + jnp.arange(block_size, dtype=jnp.int32)[None, :]
    ).reshape(-1)
    ordered = jnp.take(rhs_in, jnp.take(pivots, row_index), axis=2)
    my_index = lax.axis_index("row")
    my_block = slot_block[my_index]
    current = lax.all_to_all(ordered, "row", split_axis=2, concat_axis=1, tiled=True)
    sections = ((panel_first, inverse_first), (panel_second, inverse_second))
    for block_step in range(2):
        panel_rows, inverse = sections[block_step]
        holder = owners[block_step]
        solved = complex_product(current, inverse)
        solution = broadcast(solved, "row", holder)
        update = complex_product(solution, panel_rows)
        current = jnp.where(my_block > block_step, current - update, current)
        current = jnp.where(my_block == block_step, solution, current)
    return current


def solution(mesh):
    return jax.shard_map(
        shards,
        mesh=mesh,
        in_specs=(
            P(None, ("rhs", "row"), None),
            P(),
            P(),
            P(None, "row", None),
            P(None, "row", None),
            P(),
            P(),
        ),
        out_specs=P(None, "rhs", "row"),
        check_vma=False,
    )
```

profile of v0, /device:TPU:1, one launch (start us, length us, event | category | flops | bytes accessed | tf_op | source)
XLA Modules:
  0.0 983.9 jit_solution(494485509080680540)
XLA Ops:
  6.5 0.7 compare_select_fusion.4
  7.2 0.7 scatter_custom_fusion
  7.9 0.1 fusion.51
  8.0 0.1 copy.12
  8.1 0.1 compare_select_fusion.1
  8.2 90.5 %gather_fusion = s32[16384]{0:T(1024)S(1)} fusion(s32[16384]{0:T(1024)S(1)} %copy-done, s32[16384]{0:T(1024)S(1)} %broadcast_clamp_fusion.1), kind=kCustom, calls=%fused_computation | custom fusion | bytes 196608 | tf_op jit(solution)/shard_map/jit(_take)/gather | solution.py:36
  98.8 0.2 compare_select_fusion
  99.0 14.8 %copy.9 = f32[2,4,16384]{1,0,2:T(2,128)} copy(f32[2,4,16384]{2,1,0:T(4,128)S(1)} %copy-done.8) | data formatting | bytes 1048576 | tf_op args[0]
  113.9 118.0 %gather_fusion.1 = f32[16384,2,4]{2,1,0:T(2,128)} fusion(f32[2,4,16384]{1,0,2:T(2,128)} %copy.9, s32[16384]{0:T(1024)S(1)} %broadcast_clamp_fusion), kind=kCustom, calls=%fused_computation.1 | custom fusion | bytes 1114112 | tf_op jit(solution)/shard_map/jit(_take)/gather | solution.py:36
  231.9 59.0 %fusion.56 = f32[16384,2,4]{2,1,0:T(2,128)} fusion(f32[16384,2,4]{2,1,0:T(2,128)} %gather_fusion.1, pred[16384]{0:T(1024)(128)(4,1)S(1)} %compare_and_fusion), kind=kLoop, calls=%fused_computation.89 | loop fusion | flops 131072 | bytes 1064960
  290.9 27.6 %reshape.122 = f32[32,1,4096]{2,1,0:T(1,128)} reshape(f32[16384,2,4]{2,1,0:T(2,128)} %fusion.56) | data formatting | bytes 1048576
  318.5 10.0 %all-to-all-start = ((f32[32,1,4096]{2,1,0:T(1,128)}), f32[32,1,4096]{2,1,0:T(1,128)S(1)}, u32[]{:S(2)}, u32[]{:S(2)}) async-start(f32[32,1,4096]{2,1,0:T(1,128)} %reshape.122), calls=%async_computation | async-start | bytes 1048576 | tf_op jit(solution)/shard_map/all_to_all | solution.py:39
  328.6 0.2 all-reduce.3.cloned.1.call-start
  328.8 0.6 fusion.55
  330.1 14.9 %all-to-all-done = f32[32,1,4096]{2,1,0:T(1,128)S(1)} async-done(((f32[32,1,4096]{2,1,0:T(1,128)}), f32[32,1,4096]{2,1,0:T(1,128)S(1)}, u32[]{:S(2)}, u32[]{:S(2)}) %all-to-all-start) | async-done | bytes 524320 | tf_op jit(solution)/shard_map/all_to_all | solution.py:39
  345.0 0.5 broadcast.121
  345.5 1.9 reduce
  347.4 27.8 %reshape.123 = f32[16384,2,4]{2,1,0:T(2,128)} reshape(f32[32,4096]{1,0:T(8,128)S(1)} %reduce) | data formatting | bytes 1048576
  375.2 19.1 %copy.10 = f32[2,4,32,512]{3,1,2,0:T(4,128)S(1)} copy(f32[2,4,32,512]{1,0,3,2:T(2,128)} %bitcast.111) | data formatting | bytes 1048576 | tf_op jit(solution)/shard_map/all_to_all | solution.py:39
  394.4 0.7 fusion.54
  395.1 0.1 squeeze.73
  395.2 1.2 fusion.26
  396.4 1.2 fusion.30
  397.6 1.0 squeeze.75
  398.6 1.2 fusion.7
  399.8 1.2 fusion.6
  401.0 0.8 maximum_select_fusion
  401.9 0.3 all-reduce.5.cloned.1.call-start
  402.1 0.6 dynamic_slice.3
  404.5 0.2 all_to_all.16
  404.7 274.4 %all-reduce.3.cloned.1.call-done = f32[2,128,512]{2,1,0:T(8,128)} async-done(((f32[2,128,512]{2,1,0:T(8,128)}), f32[2,128,512]{2,1,0:T(8,128)}) %all-reduce.3.cloned.1.call-update) | async-done | bytes 524304 | tf_op jit(solution)/shard_map/psum | solution.py:9
  679.1 2.2 fusion.20
  681.3 2.1 fusion.24
  683.4 1.2 fusion.4
  684.6 1.2 fusion.5
  685.8 0.2 fusion.48
  686.0 0.2 copy-done.4
  686.2 1.2 fusion.14
  687.4 1.2 fusion.18
  688.5 1.2 fusion.2
  689.7 1.2 fusion.3
  690.9 0.8 maximum_select_fusion.1
  692.9 276.4 %all-reduce.5.cloned.1.call-done = f32[2,128,512]{2,1,0:T(8,128)} async-done(((f32[2,128,512]{2,1,0:T(8,128)}), f32[2,128,512]{2,1,0:T(8,128)}) %all-reduce.5.cloned.1.call-update) | async-done | bytes 524304 | tf_op jit(solution)/shard_map/psum | solution.py:9
  969.4 2.2 fusion.8
  971.6 2.1 fusion.12
  973.8 1.2 fusion
  974.9 1.2 fusion.1
  976.1 1.0 fusion.49
  (27 shorter events, 0.2 us)
Async XLA Ops:
  6.5 1.7 copy-start
  8.2 90.8 %copy-start.8 = (f32[2,4,16384]{2,1,0:T(4,128)S(1)}, f32[2,4,16384]{2,1,0:T(4,128)}, u32[]{:S(2)}) copy-start(f32[2,4,16384]{2,1,0:T(4,128)} %param.7) | copy-start | bytes 1572868
  290.9 37.9 %copy-start.9 = (s32[32]{0:T(128)S(1)}, s32[32]{0:T(128)}, u32[]{:S(2)}) copy-start(s32[32]{0:T(128)} %param.9) | copy-start | bytes 388
  318.5 26.4 %all-to-all-start = ((f32[32,1,4096]{2,1,0:T(1,128)}), f32[32,1,4096]{2,1,0:T(1,128)S(1)}, u32[]{:S(2)}, u32[]{:S(2)}) async-start(f32[32,1,4096]{2,1,0:T(1,128)} %reshape.122), calls=%async_computation | async-start | bytes 1048576 | tf_op jit(solution)/shard_map/all_to_all | solution.py:39
  328.6 350.5 %all-reduce.3.cloned.1.call-start = ((), (), s32[]{:S(2)}) async-start(), calls=%async_computation.1 | async-start | bytes 1048576 | tf_op jit(solution)/shard_map/psum | solution.py:9
  375.2 20.0 %copy-start.2 = (f32[2,512,512]{2,1,0:T(8,128)S(1)}, f32[2,512,512]{2,1,0:T(8,128)}, u32[]{:S(2)}) copy-start(f32[2,512,512]{2,1,0:T(8,128)} %param.12) | copy-start | bytes 6291460
  401.0 278.1 %copy-start.3 = (f32[2,512,512]{2,1,0:T(8,128)S(1)}, f32[2,512,512]{2,1,0:T(8,128)}, u32[]{:S(2)}) copy-start(f32[2,512,512]{2,1,0:T(8,128)} %param.10) | copy-start | bytes 6291460
  401.9 567.5 %all-reduce.5.cloned.1.call-start = ((), (), s32[]{:S(2)}) async-start(), calls=%async_computation.2 | async-start | bytes 1048576 | tf_op jit(solution)/shard_map/psum | solution.py:9
  679.1 4.3 copy-start.6
  684.6 1.6 copy-start.4
  689.7 279.7 %copy-start.5 = (f32[2,512,512]{2,1,0:T(8,128)S(1)}, f32[2,512,512]{2,1,0:T(8,128)}, u32[]{:S(2)}) copy-start(f32[2,512,512]{2,1,0:T(8,128)} %param.11) | copy-start | bytes 6291460
  969.4 4.3 copy-start.7
  973.7 3.3 copy-start.1
Sparse Core Ops, SparseCore 0:
  402.0 277.0 all-reduce.2
  691.9 277.4 all-reduce.4
where the time goes:
time: 985 us; the launch traced here: 984 us
  waiting for transfers between devices  566 us (57%)
  local copies, waits for them, and re-layouts  303 us (31%)
  other arithmetic  64.8 us (7%)
  matrix products  22.7 us (2%)
  between operations  17.3 us (2%)
  starting transfers between devices  10.5 us (1%)
    psum x2, waiting for transfers between devices, broadcast(): return lax.psum(jnp.where(mine, shard, jnp.zeros_like(shard)), axis)  551 us
    gather x2, local copies, waits for them, and re-layouts, shards(): ordered = jnp.take(rhs_in, jnp.take(pivots, row_index), axis=2)  209 us
    unnamed x25, local copies, waits for them, and re-layouts  70.7 us
    unnamed x2, other arithmetic  59.1 us
    dot_general x16, matrix products, multiply(): lax.dot_general(first, second, contract, precision=lax.Precision.HIGHEST,...  22.7 us
    all_to_all x3, local copies, waits for them, and re-layouts, shards(): lax.all_to_all(ordered, 'row', split_axis=2, concat_axis=1, tiled=True)  19.8 us
  transfers between devices with their start and end apart: 3, of which 3 were waited for; matrix products, arithmetic and copies ran while one was open for 0% of the time, Pallas kernels for 0%

commit v1 on v0

--- a/solution.py
+++ b/solution.py
@@ -6,7 +6,7 @@
 
 def broadcast(shard, axis, root):
     mine = lax.axis_index(axis) == root
-    return lax.psum(jnp.where(mine, shard, jnp.zeros_like(shard)), axis)
+    return jnp.sum(lax.all_gather(jnp.where(mine, shard, jnp.zeros_like(shard)), axis), axis=0)
 
 
 def complex_product(operand, matrix):

time: 985 us -> 640 us (0.65)
  waiting for transfers between devices: 566 us -> 210 us
  other arithmetic: 64.8 us -> 80.2 us
    psum x2 -> x0, waiting for transfers between devices: 551 us -> none  [broadcast(): return lax.psum(jnp.where(mine, shard, jnp.zeros_like(shard)), axis)]
    all_gather x0 -> x2, waiting for transfers between devices: none -> 195 us  [broadcast(): lax.all_gather(jnp.where(mine, shard, jnp.zeros_like(shard)), axis)]
    reduce_sum x0 -> x2, other arithmetic: none -> 15.5 us  [broadcast(): jnp.sum(lax.all_gather(jnp.where(mine, shard, jnp.zeros_like(shard)), axi...]
    unnamed x25 -> x23, local copies, waits for them, and re-layouts: 70.7 us -> 70.7 us
where the time goes in v1:
time: 640 us
  local copies, waits for them, and re-layouts  303 us (47%)
  waiting for transfers between devices  210 us (33%)
  other arithmetic  80.2 us (13%)
  matrix products  19.1 us (3%)
  between operations  17.3 us (3%)
  starting transfers between devices  10.5 us (2%)
    gather x2, local copies, waits for them, and re-layouts, shards(): ordered = jnp.take(rhs_in, jnp.take(pivots, row_index), axis=2)  208 us
    all_gather x2, waiting for transfers between devices, broadcast(): lax.all_gather(jnp.where(mine, shard, jnp.zeros_like(shard)), axis)  195 us
    unnamed x23, local copies, waits for them, and re-layouts  70.7 us
    unnamed x2, other arithmetic  59.1 us
    all_to_all x3, local copies, waits for them, and re-layouts, shards(): lax.all_to_all(ordered, 'row', split_axis=2, concat_axis=1, tiled=True)  20.6 us
    dot_general x16, matrix products, multiply(): lax.dot_general(first, second, contract, precision=lax.Precision.HIGHEST,...  19.1 us
    reduce_sum x2, other arithmetic, broadcast(): jnp.sum(lax.all_gather(jnp.where(mine, shard, jnp.zeros_like(shard)), axi...  15.5 us
    all_to_all x1, waiting for transfers between devices, shards(): lax.all_to_all(ordered, 'row', split_axis=2, concat_axis=1, tiled=True)  15 us
  transfers between devices with their start and end apart: 3, of which 3 were waited for; matrix products, arithmetic and copies ran while one was open for 0% of the time, Pallas kernels for 0%

profile of v1, /device:TPU:1, one launch (start us, length us, event | category | flops | bytes accessed | tf_op | source)
XLA Modules:
  0.0 639.6 jit_solution(5274886086589267824)
XLA Ops:
  6.5 0.7 compare_select_fusion.4
  7.2 0.7 scatter_custom_fusion
  7.9 0.1 fusion.51
  8.2 90.5 %gather_fusion = s32[16384]{0:T(1024)S(1)} fusion(s32[16384]{0:T(1024)S(1)} %copy-done, s32[16384]{0:T(1024)S(1)} %broadcast_clamp_fusion.1), kind=kCustom, calls=%fused_computation | custom fusion | bytes 196608 | tf_op jit(solution)/shard_map/jit(_take)/gather | solution.py:36
  98.8 0.2 compare_select_fusion
  99.0 14.9 %copy.11 = f32[2,4,16384]{1,0,2:T(2,128)} copy(f32[2,4,16384]{2,1,0:T(4,128)S(1)} %copy-done.7) | data formatting | bytes 1048576 | tf_op args[0]
  113.9 117.4 %gather_fusion.1 = f32[16384,2,4]{2,1,0:T(2,128)} fusion(f32[2,4,16384]{1,0,2:T(2,128)} %copy.11, s32[16384]{0:T(1024)S(1)} %broadcast_clamp_fusion), kind=kCustom, calls=%fused_computation.1 | custom fusion | bytes 1114112 | tf_op jit(solution)/shard_map/jit(_take)/gather | solution.py:36
  231.3 59.0 %fusion.56 = f32[16384,2,4]{2,1,0:T(2,128)} fusion(f32[16384,2,4]{2,1,0:T(2,128)} %gather_fusion.1, pred[16384]{0:T(1024)(128)(4,1)S(1)} %compare_and_fusion), kind=kLoop, calls=%fused_computation.89 | loop fusion | flops 131072 | bytes 1064960
  290.3 27.6 %reshape.184 = f32[32,1,4096]{2,1,0:T(1,128)} reshape(f32[16384,2,4]{2,1,0:T(2,128)} %fusion.56) | data formatting | bytes 1048576
  317.9 10.0 %all-to-all-start = ((f32[32,1,4096]{2,1,0:T(1,128)}), f32[32,1,4096]{2,1,0:T(1,128)S(1)}, u32[]{:S(2)}, u32[]{:S(2)}) async-start(f32[32,1,4096]{2,1,0:T(1,128)} %reshape.184), calls=%async_computation | async-start | bytes 1048576 | tf_op jit(solution)/shard_map/all_to_all | solution.py:39
  328.0 0.2 all-gather.3.cloned.1.call-start
  328.2 0.6 fusion.55
  329.4 15.0 %all-to-all-done = f32[32,1,4096]{2,1,0:T(1,128)S(1)} async-done(((f32[32,1,4096]{2,1,0:T(1,128)}), f32[32,1,4096]{2,1,0:T(1,128)S(1)}, u32[]{:S(2)}, u32[]{:S(2)}) %all-to-all-start) | async-done | bytes 524320 | tf_op jit(solution)/shard_map/all_to_all | solution.py:39
  344.4 0.5 broadcast.149
  344.9 1.9 reduce
  346.8 27.8 %reshape.185 = f32[16384,2,4]{2,1,0:T(2,128)} reshape(f32[32,4096]{1,0:T(8,128)S(1)} %reduce) | data formatting | bytes 1048576
  374.6 19.1 %copy.12 = f32[2,4,32,512]{3,1,2,0:T(4,128)S(1)} copy(f32[2,4,32,512]{1,0,3,2:T(2,128)} %bitcast.111) | data formatting | bytes 1048576 | tf_op jit(solution)/shard_map/all_to_all | solution.py:39
  393.8 0.7 fusion.54
  394.5 0.1 squeeze.73
  394.6 1.2 fusion.26
  395.8 1.2 fusion.30
  397.0 1.0 squeeze.75
  398.0 1.2 fusion.7
  399.2 1.2 fusion.6
  400.4 0.8 maximum_select_fusion
  401.3 0.3 all-gather.5.cloned.1.call-start
  401.5 0.6 dynamic_slice.3
  403.9 1.0 all_to_all.16
  404.9 95.0 %all-gather.3.cloned.1.call-done = f32[32,2,128,512]{3,2,1,0:T(8,128)} async-done(((f32[1,2,128,512]{3,2,1,0:T(8,128)}), f32[32,2,128,512]{3,2,1,0:T(8,128)}) %all-gather.3.cloned.1.call-update) | async-done | bytes 16777232 | tf_op jit(solution)/shard_map/all_gather | solution.py:9
  499.9 7.8 %reduce_sum.18 = f32[2,128,512]{2,1,0:T(8,128)S(1)} reduce(f32[32,2,128,512]{3,2,1,0:T(8,128)} %all-gather.3.cloned.1.call-done, f32[]{:T(128)} %constant.51.clone.1), dimensions={0}, to_apply=%region_1.2 | reduce | flops 4063232 | bytes 17301508 | tf_op jit(solution)/shard_map/reduce_sum | solution.py:9
  507.6 1.2 fusion.20
  508.8 1.2 fusion.24
  510.0 1.2 fusion.4
  511.2 1.2 fusion.5
  512.4 0.2 fusion.48
  512.6 0.2 copy-done.4
  512.8 1.2 fusion.14
  514.0 1.2 fusion.18
  515.2 1.2 fusion.2
  516.3 1.2 fusion.3
  517.5 0.8 maximum_select_fusion.1
  519.5 99.5 %all-gather.5.cloned.1.call-done = f32[32,2,128,512]{3,2,1,0:T(8,128)} async-done(((f32[1,2,128,512]{3,2,1,0:T(8,128)}), f32[32,2,128,512]{3,2,1,0:T(8,128)}) %all-gather.5.cloned.1.call-update) | async-done | bytes 16777232 | tf_op jit(solution)/shard_map/all_gather | solution.py:9
  619.1 7.8 %reduce_sum.19 = f32[2,128,512]{2,1,0:T(8,128)S(1)} reduce(f32[32,2,128,512]{3,2,1,0:T(8,128)} %all-gather.5.cloned.1.call-done, f32[]{:T(128)} %constant.51.clone.1), dimensions={0}, to_apply=%region_2.3 | reduce | flops 4063232 | bytes 17301508 | tf_op jit(solution)/shard_map/reduce_sum | solution.py:9
  626.8 1.4 fusion.8
  628.3 1.2 fusion.12
  629.5 1.2 fusion
  630.6 1.2 fusion.1
  631.8 1.0 fusion.49
  (27 shorter events, 0.3 us)
Async XLA Ops:
  6.5 1.7 copy-start
  8.2 90.8 %copy-start.7 = (f32[2,4,16384]{2,1,0:T(4,128)S(1)}, f32[2,4,16384]{2,1,0:T(4,128)}, u32[]{:S(2)}) copy-start(f32[2,4,16384]{2,1,0:T(4,128)} %param.7) | copy-start | bytes 1572868
  290.3 37.9 %copy-start.8 = (s32[32]{0:T(128)S(1)}, s32[32]{0:T(128)}, u32[]{:S(2)}) copy-start(s32[32]{0:T(128)} %param.9) | copy-start | bytes 388
  317.9 26.4 %all-to-all-start = ((f32[32,1,4096]{2,1,0:T(1,128)}), f32[32,1,4096]{2,1,0:T(1,128)S(1)}, u32[]{:S(2)}, u32[]{:S(2)}) async-start(f32[32,1,4096]{2,1,0:T(1,128)} %reshape.184), calls=%async_computation | async-start | bytes 1048576 | tf_op jit(solution)/shard_map/all_to_all | solution.py:39
  328.0 171.9 %all-gather.3.cloned.1.call-start = ((), (), s32[]{:S(2)}) async-start(), calls=%async_computation.1 | async-start | bytes 17301504 | tf_op jit(solution)/shard_map/all_gather | solution.py:9
  374.6 20.0 %copy-start.2 = (f32[2,512,512]{2,1,0:T(8,128)S(1)}, f32[2,512,512]{2,1,0:T(8,128)}, u32[]{:S(2)}) copy-start(f32[2,512,512]{2,1,0:T(8,128)} %param.12) | copy-start | bytes 6291460
  401.3 217.8 %all-gather.5.cloned.1.call-start = ((), (), s32[]{:S(2)}) async-start(), calls=%async_computation.2 | async-start | bytes 17301504 | tf_op jit(solution)/shard_map/all_gather | solution.py:9
  404.9 102.7 %copy-start.3 = (f32[2,512,512]{2,1,0:T(8,128)S(1)}, f32[2,512,512]{2,1,0:T(8,128)}, u32[]{:S(2)}) copy-start(f32[2,512,512]{2,1,0:T(8,128)} %param.10) | copy-start | bytes 6291460
  510.0 2.4 copy-start.6
  511.2 1.6 copy-start.4
  519.5 107.3 %copy-start.5 = (f32[2,512,512]{2,1,0:T(8,128)S(1)}, f32[2,512,512]{2,1,0:T(8,128)}, u32[]{:S(2)}) copy-start(f32[2,512,512]{2,1,0:T(8,128)} %param.11) | copy-start | bytes 6291460
  629.4 3.3 copy-start.1
Sparse Core Ops, SparseCore 0:
  401.4 98.4 all-gather.2
  518.5 100.5 all-gather.4
